TPU v7x, 32 devices: a whole 2x2x4 slice. The times are simulated.
32 devices in a mesh: groups: 2 (over y), head: 4 (over z), hist: 4 (over x, core).
Axes of the slice: x: 2, y: 2, z: 4, core: 2. Of those that a mesh axis runs over, the one named last changes fastest.
Arguments:
- tokens: bfloat16 [1024, 8192], P('groups', 'hist'), parts along dimension 0, may hold values from -6 to 6
- w_qkvu: bfloat16 [8192, 4, 8192], P('hist', None, 'head'), may hold values from -0.0625 to 0.0625
- k_cache: bfloat16 [4096, 8192], P(('groups', 'hist'), 'head'), parts along dimension 0, may hold values from -6 to 6
- v_cache: bfloat16 [4096, 8192], P(('groups', 'hist'), 'head'), parts along dimension 0
- w_out: bfloat16 [8192, 8192], P('head', 'hist'), may hold values from -0.0625 to 0.0625
- vis_start: int32 [1024], P('groups'), parts along dimension 0, may hold values from 0 to 511, as said below
- vis_end: int32 [1024], P('groups'), parts along dimension 0, may hold values from 1025 to 2048
Outputs:
- layer_out: bfloat16 [1024, 8192], P(('groups', 'head'), 'hist'), parts along dimension 0
There are 2 independent parts, one for each index of `groups`. A program takes and returns all parts, laid end to end along the dimension named above; an argument that names none is the same for every part. Nothing has to cross between parts.
Inputs may be any that keep to these rules, and one draw needn't show every extreme that they name: vis_start and vis_end together leave every candidate 2048 // 4 + 2 or more visible history events.
All inputs are finite; a program needn't handle non-finite values.
Results may differ from a plain program's by a relative error of at most 0.02.
Values may be sent and summed in bfloat16 or wider, within the bound.
A program may use at most 192 MiB of HBM per device.

v0:
```python
import jax
import jax.numpy as jnp
from jax import lax
from jax.sharding import PartitionSpec as P

DH = 128


epsilon = 1e-05


def history_terms(query_heads, key_block, value_block, vis_lo, vis_hi):
    head_total = query_heads.shape[1]
    head_size = query_heads.shape[2]
    block_len = key_block.shape[0]
    key_heads = key_block.reshape(block_len, head_total, head_size)
    value_heads = value_block.reshape(block_len, head_total, head_size)
    scores = jnp.einsum(
        "rhe,lhe->rhl", query_heads, key_heads, preferred_element_type=jnp.float32
    ) * head_size ** (-0.5)
    positions = lax.iota(jnp.int32, block_len)
    visible = (positions[None, :] >= vis_lo[:, None]) & (positions[None, :] < vis_hi[:, None])
    weights = jnp.where(visible[:, None, :], jax.nn.silu(scores), 0.0).astype(jnp.bfloat16)
    summed_values = jnp.einsum(
        "rhl,lhe->rhe", weights, value_heads, preferred_element_type=jnp.float32
    )
    return summed_values.reshape(query_heads.shape[0], head_total * head_size)


def local(tokens, w_qkvu, k_cache, v_cache, w_out, vis_start, vis_end):
    cand_total = tokens.shape[0]
    hist_count = lax.axis_size("hist")
    head_count = lax.axis_size("head")
    own_count = cand_total // hist_count
    own_first = lax.axis_index("hist") * own_count
    local_width = w_qkvu.shape[2]
    local_heads = local_width // DH
    full_width = local_width * head_count
    flat_weight = w_qkvu.reshape(w_qkvu.shape[0], 4 * local_width)
    start_own = lax.dynamic_slice_in_dim(vis_start, own_first, own_count)
    end_own = lax.dynamic_slice_in_dim(vis_end, own_first, own_count)
    summed = lax.psum_scatter(
        jnp.dot(tokens, flat_weight, preferred_element_type=jnp.float32).astype(jnp.bfloat16),
        "hist",
        scatter_dimension=0,
        tiled=True,
    ).astype(jnp.float32)
    own_part = jax.nn.silu(summed).astype(jnp.bfloat16).reshape(own_count, 4, local_width)
    own_query = own_part[:, 0]
    own_key = own_part[:, 1]
    own_value = own_part[:, 2]
    own_gate = own_part[:, 3]
    query_heads = own_query.reshape(own_count, local_heads, DH)
    history = history_terms(
        query_heads,
        lax.all_gather(k_cache, "hist", axis=0, tiled=True),
        lax.all_gather(v_cache, "hist", axis=0, tiled=True),
        start_own,
        end_own,
    )
    counts = (end_own - start_own).astype(jnp.float32)
    own_product = own_query.astype(jnp.float32) * own_key.astype(jnp.float32)
    own_score = jnp.sum(own_product.reshape(own_count, local_heads, DH), axis=2) * DH ** (-0.5)
    own_term = jax.nn.silu(own_score)[:, :, None] * own_value.astype(jnp.float32).reshape(
        own_count, local_heads, DH
    )
    attended = history / jnp.sqrt(counts)[:, None] + own_term.reshape(own_count, local_width)
    row_sum = lax.psum(jnp.sum(attended, axis=1), "head")
    centered = attended - (row_sum / full_width)[:, None]
    spread = lax.psum(jnp.sum(centered * centered, axis=1), "head")
    normed = centered * lax.rsqrt(spread / full_width + epsilon)[:, None]
    gated_rows = (normed * own_gate.astype(jnp.float32)).astype(jnp.bfloat16)
    gathered = lax.all_gather(gated_rows, "hist", axis=0, tiled=True)
    out_count = cand_total // head_count
    out_first = lax.axis_index("head") * out_count
    whole_out = jnp.dot(gathered, w_out, preferred_element_type=jnp.float32)
    total_out = lax.psum(whole_out.astype(jnp.bfloat16), "head").astype(jnp.float32)
    summed_out = lax.dynamic_slice_in_dim(total_out, out_first, out_count, 0)
    residual = lax.dynamic_slice_in_dim(tokens, out_first, out_count, 0).astype(jnp.float32)
    return (residual + summed_out).astype(jnp.bfloat16)


def solution(mesh):
    in_specs = (
        P("groups", "hist"),
        P("hist", None, "head"),
        P(("groups", "hist"), "head"),
        P(("groups", "hist"), "head"),
        P("head", "hist"),
        P("groups"),
        P("groups"),
    )
    out_specs = P(("groups", "head"), "hist")
    return jax.shard_map(local, mesh=mesh, in_specs=in_specs, out_specs=out_specs, check_vma=False)
```

profile of v0, /device:TPU:7, one launch (start us, length us, event | category | flops | bytes accessed | tf_op | source)
XLA Modules:
  0.0 365.5 jit_solution(18409414456210205719)
XLA Ops:
  6.5 0.7 all-gather.6.cloned.1.call-update
  7.3 30.2 %copy.29 = bf16[256,8,4,2048]{3,1,2,0:T(8,128)(2,1)} copy(bf16[256,8,4,2048]{3,2,1,0:T(4,128)(2,1)} %bitcast.58) | data formatting | bytes 67108864
  37.5 25.5 %convolution_convert_fusion = bf16[512,8192]{1,0:T(8,128)(2,1)} fusion(bf16[512,2048]{1,0:T(8,128)(2,1)S(1)} %copy-done.2, bf16[2048,8192]{1,0:T(8,128)(2,1)} %bitcast.59), kind=kOutput, calls=%fused_computation.7 | convolution fusion | flops 17184063488 | bytes 44040192 | tf_op jit(solution)/shard_map/dot_general | solution.py:43
  63.1 1.5 copy-done.1
  64.6 2.5 copy.14
  67.2 0.2 all-gather.8.cloned.1.call-start
  67.4 0.8 convert_sqrt_fusion
  68.2 0.5 fusion.19
  68.7 12.5 %copy.17 = bf16[2048,2048]{0,1:T(8,128)(2,1)} copy(bf16[2048,2048]{1,0:T(8,128)(2,1)} %all-gather.6.cloned.1.call-done) | data formatting | bytes 16777216 | tf_op jit(solution)/shard_map/all_gather | solution.py:57
  81.2 60.2 %reduce-scatter.2.cloned.1.call-done = bf16[128,8192]{1,0:T(8,128)(2,1)} async-done(((bf16[512,8192]{1,0:T(8,128)(2,1)}), bf16[128,8192]{1,0:T(8,128)(2,1)}) %reduce-scatter.2.cloned.1.call-update) | async-done | bytes 2097168 | tf_op jit(solution)/shard_map/reduce_scatter | solution.py:42
  141.3 4.0 %fusion.12 = bf16[128,8192]{1,0:T(8,128)(2,1)} fusion(bf16[128,8192]{1,0:T(8,128)(2,1)} %reduce-scatter.2.cloned.1.call-done), kind=kLoop, calls=%fused_computation.15 | loop fusion | flops 6291456 | bytes 4194304 | tf_op jit(solution)/shard_map/convert_element_type | solution.py:48
  145.4 3.3 reshape.92
  148.7 4.4 %fusion.24 = (bf16[128,1,2048]{2,1,0:T(2,128)(2,1)S(1)}, bf16[128,1,2048]{2,1,0:T(2,128)(2,1)}, f32[128,1,2048]{2,1,0:T(1,128)}, bf16[128,1,2048]{2,1,0:T(2,128)(2,1)}) fusion(bf16[128,4,2048]{2,1,0:T(4,128)(2,1)S(1)} %reshape.92), kind=kLoop, calls=%fused_computation.42 | loop fusion | flops 262144 | bytes 4718592 | tf_op jit(solution)/shard_map/slice | solution.py:51
  153.0 2.5 copy.27
  155.5 2.5 copy.26
  158.0 0.2 fusion.14
  158.2 0.6 copy-done
  158.9 1.3 copy.21
  160.2 0.4 copy_convert_fusion
  160.6 0.3 copy.22
  160.9 40.9 %all-gather.4.cloned.1.call-done = bf16[2048,2048]{0,1:T(8,128)(2,1)} async-done(((bf16[512,2048]{0,1:T(8,128)(2,1)}), bf16[2048,2048]{0,1:T(8,128)(2,1)}) %all-gather.4.cloned.1.call-update) | async-done | bytes 8388624 | tf_op jit(solution)/shard_map/all_gather | solution.py:56
  201.8 11.9 %fusion.23 = (f32[128]{0:T(128)S(1)}, f32[16,128,128]{1,2,0:T(8,128)S(1)}) fusion(f32[128,16,128]{0,2,1:T(8,128)S(1)} %bitcast.61, f32[128,16]{0,1:T(8,128)S(1)} %divide_multiply_fusion, f32[128]{0:T(128)S(1)} %get-tuple-element.5, bf16[2048,16,128]{0,2,1:T(8,128)(2,1)} %bitcast.60, pred[128,2048]{1,0:T(8,128)(4,1)S(1)} %fusion.19, ...), kind=kOutput, calls=%fused_computation.41 | convolution fusion | flops 2177892352 | bytes 19670016 | tf_op jit(solution)/shard_map/rhl,lhe->rhe/dot_general | solution.py:24
  213.7 1.3 copy.18
  215.0 9.7 %psum.21 = f32[128]{0:T(128)S(1)} all-reduce(f32[128]{0:T(128)S(1)} %get-tuple-element.12), channel_id=1, replica_groups=mesh['groups'=2,'head'=4,'hist'=4] {'head'}, use_global_device_ids=true, to_apply=%region_3.4 | all-reduce | flops 128 | bytes 1024 | tf_op jit(solution)/shard_map/psum | solution.py:68
  224.7 0.3 multiply_reduce_fusion
  225.0 6.6 %psum.22 = f32[128]{0:T(128)S(1)} all-reduce(f32[128]{0:T(128)S(1)} %multiply_reduce_fusion), channel_id=1, replica_groups=mesh['groups'=2,'head'=4,'hist'=4] {'head'}, use_global_device_ids=true, to_apply=%region_5.6 | all-reduce | flops 128 | bytes 1024 | tf_op jit(solution)/shard_map/psum | solution.py:70
  231.6 3.7 %fusion.13 = bf16[128,2048]{1,0:T(8,128)(2,1)} fusion(f32[128,1,2048]{2,1,0:T(1,128)} %get-tuple-element.10, f32[128,2048]{1,0:T(8,128)} %copy.21, f32[128,2048]{1,0:T(8,128)} %copy.18, f32[128]{0:T(128)S(1)} %add_rsqrt_fusion, f32[128]{0:T(128)S(1)} %broadcast_multiply_fusion, f32[128]{0:T(128)S(1)} %get-tuple-element.5, ...), kind=kLoop, calls=%fused_computation.19 | loop fusion | flops 2097152 | bytes 4195840 | tf_op jit(solution)/shard_map/convert_element_type | solution.py:72
  235.3 0.3 all-reduce.2.cloned.1.call-start
  235.6 24.9 %all-gather.8.cloned.1.call-done = bf16[512,2048]{1,0:T(8,128)(2,1)} async-done(((bf16[128,2048]{1,0:T(8,128)(2,1)}), bf16[512,2048]{1,0:T(8,128)(2,1)}) %all-gather.8.cloned.1.call-update) | async-done | bytes 2097168 | tf_op jit(solution)/shard_map/all_gather | solution.py:73
  260.5 9.9 %convolution_convert_fusion.1 = bf16[512,2048]{1,0:T(8,128)(2,1)} fusion(bf16[512,2048]{1,0:T(8,128)(2,1)} %all-gather.8.cloned.1.call-done, bf16[2048,2048]{1,0:T(8,128)(2,1)} %param.11), kind=kOutput, calls=%fused_computation.16 | convolution fusion | flops 4296015872 | bytes 12582912 | tf_op jit(solution)/shard_map/dot_general | solution.py:76
  270.4 86.5 %all-reduce.2.cloned.1.call-done = bf16[512,2048]{1,0:T(8,128)(2,1)} async-done(((bf16[512,2048]{1,0:T(8,128)(2,1)}), bf16[512,2048]{1,0:T(8,128)(2,1)}) %all-reduce.2.cloned.1.call-update) | async-done | bytes 2097168 | tf_op jit(solution)/shard_map/psum | solution.py:77
  356.8 2.1 add_convert_fusion
  (16 shorter events, 0.3 us)
Async XLA Ops:
  6.5 62.2 %all-gather.6.cloned.1.call-start = ((), (), s32[]{:S(2)}) async-start(), calls=%async_computation.3 | async-start | bytes 10485760 | tf_op jit(solution)/shard_map/all_gather | solution.py:57
  7.3 134.1 %reduce-scatter.2.cloned.1.call-start = ((), (), s32[]{:S(2)}) async-start(), calls=%async_computation.1 | async-start | bytes 10485760 | tf_op jit(solution)/shard_map/reduce_scatter | solution.py:42
  7.3 30.2 %copy-start.2 = (bf16[512,2048]{1,0:T(8,128)(2,1)S(1)}, bf16[512,2048]{1,0:T(8,128)(2,1)}, u32[]{:S(2)}) copy-start(bf16[512,2048]{1,0:T(8,128)(2,1)} %param.7) | copy-start | bytes 6291460
  63.0 1.6 copy-start.1
  63.0 138.7 %all-gather.4.cloned.1.call-start = ((), (), s32[]{:S(2)}) async-start(), calls=%async_computation.2 | async-start | bytes 10485760 | tf_op jit(solution)/shard_map/all_gather | solution.py:56
  67.2 193.3 %all-gather.8.cloned.1.call-start = ((), (), s32[]{:S(2)}) async-start(), calls=%async_computation.4 | async-start | bytes 2621440 | tf_op jit(solution)/shard_map/all_gather | solution.py:73
  158.0 0.8 copy-start
  235.3 121.5 %all-reduce.2.cloned.1.call-start = ((), (), s32[]{:S(2)}) async-start(), calls=%async_computation.5 | async-start | bytes 4194304 | tf_op jit(solution)/shard_map/psum | solution.py:77
Sparse Core Ops, SparseCore 0:
  8.9 58.9 all-gather.5
  70.5 70.8 reduce-scatter.1
  142.9 58.8 all-gather.3
  235.5 24.9 all-gather.7
  270.5 86.2 all-reduce.1
where the time goes:
time: 368 us; the launch traced here: 365 us
  waiting for transfers between devices  213 us (58%)
  local copies, waits for them, and re-layouts  58.6 us (16%)
  matrix products  47.3 us (13%)
  other arithmetic  16.3 us (4%)
  blocking collectives  16.3 us (4%)
  between operations  13.3 us (4%)
    psum x1, waiting for transfers between devices, local(): lax.psum(whole_out.astype(jnp.bfloat16), 'head').astype(jnp.float32)  86.5 us
    reduce_scatter x1, waiting for transfers between devices, local(): lax.psum_scatter(jnp.dot(tokens, flat_weight, preferred_element_type=jnp....  60.2 us
    all_gather x1, waiting for transfers between devices, local(): lax.all_gather(k_cache, 'hist', axis=0, tiled=True)  40.9 us
    unnamed x10, local copies, waits for them, and re-layouts  39.8 us
    dot_general x1, matrix products, local(): jnp.dot(tokens, flat_weight, preferred_element_type=jnp.float32)  25.5 us
    all_gather x1, waiting for transfers between devices, local(): gathered = lax.all_gather(gated_rows, 'hist', axis=0, tiled=True)  24.9 us
    all_gather x1, local copies, waits for them, and re-layouts, local(): lax.all_gather(v_cache, 'hist', axis=0, tiled=True)  12.5 us
    dot_general x1, matrix products, history_terms(): jnp.einsum('rhl,lhe->rhe', weights, value_heads, preferred_element_type=j...  11.9 us
  transfers between devices with their start and end apart: 5, of which 4 were waited for; matrix products, arithmetic and copies ran while one was open for 25% of the time, Pallas kernels for 0%

commit v1 on v0

--- a/solution.py
+++ b/solution.py
@@ -1,9 +1,14 @@
+import functools
+
 import jax
 import jax.numpy as jnp
 from jax import lax
+from jax.experimental import pallas as pl
+from jax.experimental.pallas import tpu as pltpu
 from jax.sharding import PartitionSpec as P
 
 DH = 128
+TILE = 256
 
 
 epsilon = 1e-05
@@ -80,6 +85,251 @@
     return (residual + summed_out).astype(jnp.bfloat16)
 
 
+def silu(v):
+    h = 0.5 * v
+    return h + h * jnp.tanh(h)
+
+
+def history_kernel(
+    n_tiles, tok_ref, w_ref, k_ref, v_ref, lo_ref, hi_ref, att_ref, gate_ref,
+    acc, mask, mine, s1, r1, s2q, r2q, s2k, r2k, s3, r3, kv, s4, r4, part, s5, r5, ssem, rsem,
+):
+    step = pl.program_id(0)
+    me = lax.axis_index("hist")
+    x = me // 2
+    c = me % 2
+    partner = 2 * x + (1 - c)
+    across = 2 * (1 - x) + c
+    rows = tok_ref.shape[0] // 4
+    depth = tok_ref.shape[1]
+    tile = w_ref.shape[2]
+    events = k_ref.shape[0]
+
+    def quarter(xx, cc):
+        return pl.ds(pl.multiple_of((2 * xx + cc) * rows, rows), rows)
+
+    def columns(t, size, base=0):
+        return pl.ds(pl.multiple_of(t * tile + base, 128), size)
+
+    def copy(kind, src, dst, t, target):
+        return pltpu.make_async_remote_copy(
+            src_ref=src.at[t], dst_ref=dst.at[t],
+            send_sem=ssem.at[kind, t], recv_sem=rsem.at[kind, t],
+            device_id={"hist": target}, device_id_type=pl.DeviceIdType.MESH,
+        )
+
+    def copy1(t):
+        return copy(0, s1, r1, t, partner)
+
+    def copy2q(t):
+        return copy(1, s2q, r2q, t, across)
+
+    def copy2k(t):
+        return copy(2, s2k, r2k, t, across)
+
+    def copy3(t):
+        return copy(3, s3, r3, t, partner)
+
+    def copy4(t):
+        return copy(4, s4, r4, t, partner)
+
+    def copy5(t):
+        return copy(5, s5, r5, t, across)
+
+    @pl.when(step == 0)
+    def _():
+        barrier = pltpu.get_barrier_semaphore()
+        for other in (partner, across):
+            pl.semaphore_signal(
+                barrier, inc=1, device_id={"hist": other}, device_id_type=pl.DeviceIdType.MESH
+            )
+        pl.semaphore_wait(barrier, 2)
+        for half in range(2):
+            for xx in range(2):
+                q = quarter(xx, c if half == 0 else 1 - c)
+                lo = lo_ref[q, :]
+                hi = hi_ref[q, :]
+                for e in range(events // 128):
+                    pos = me * events + e * 128 + lax.broadcasted_iota(jnp.int32, lo.shape, 1)
+                    seen = (pos >= lo) & (pos < hi)
+                    mask[half, xx * rows:(xx + 1) * rows, e * 128:(e + 1) * 128] = jnp.where(
+                        seen, 1.0, 0.0
+                    )
+
+    @pl.when((step >= 5) & (step < n_tiles + 5))
+    def _():
+        t = step - 5
+        copy5(t).wait()
+        lo = lo_ref[quarter(x, c), :]
+        hi = hi_ref[quarter(x, c), :]
+        inv = lax.rsqrt((hi - lo).astype(jnp.float32))
+        for h in range(tile // DH):
+            cols = slice(h * DH, (h + 1) * DH)
+            hist = part[t, x, :, cols] + r5[t, :, cols].astype(jnp.float32)
+            q = s3[t, x, :, cols].astype(jnp.float32)
+            kk = kv[t, :, cols].astype(jnp.float32)
+            vv = kv[t, :, tile + h * DH:tile + (h + 1) * DH].astype(jnp.float32)
+            score = jnp.sum(q * kk, axis=1, keepdims=True) * DH ** (-0.5)
+            att_ref[:, columns(t, DH, h * DH)] = hist * inv + silu(score) * vv
+
+    @pl.when((step >= 4) & (step < n_tiles + 4))
+    def _():
+        t = step - 4
+        copy4(t).wait()
+        s5[t] = (part[t, 1 - x] + r4[t, 1 - x].astype(jnp.float32)).astype(jnp.bfloat16)
+        copy5(t).start()
+        part[t, x] = part[t, x] + r4[t, x].astype(jnp.float32)
+
+    @pl.when((step >= 2) & (step < n_tiles + 2))
+    def _():
+        t = step - 2
+        copy2q(t).wait()
+        s3[t] = silu(s2q[t].astype(jnp.float32) + r2q[t].astype(jnp.float32)).astype(jnp.bfloat16)
+        copy3(t).start()
+        copy2k(t).wait()
+        own = silu(mine[t, x, :, tile:].astype(jnp.float32) + r2k[t].astype(jnp.float32))
+        own = own.astype(jnp.bfloat16)
+        kv[t] = own[:, :2 * tile]
+        gate_ref[:, columns(t, tile)] = own[:, 2 * tile:]
+
+    @pl.when((step >= 1) & (step < n_tiles + 1))
+    def _():
+        t = step - 1
+        copy1(t).wait()
+        for xx in range(2):
+            both = mine[t, xx, :, :tile].astype(jnp.float32) + r1[t, xx, :, :tile].astype(jnp.float32)
+            s2q[t, xx] = both.astype(jnp.bfloat16)
+        copy2q(t).start()
+        both = mine[t, 1 - x, :, tile:].astype(jnp.float32) + r1[t, 1 - x, :, tile:].astype(jnp.float32)
+        s2k[t] = both.astype(jnp.bfloat16)
+        copy2k(t).start()
+        both = mine[t, x, :, tile:].astype(jnp.float32) + r1[t, x, :, tile:].astype(jnp.float32)
+        mine[t, x, :, tile:] = both.astype(jnp.bfloat16)
+
+    @pl.when((step >= 3) & (step < n_tiles + 3))
+    def _():
+        t = step - 3
+        copy3(t).wait()
+        for half in (1, 0):
+            src = s3 if half == 0 else r3
+            for h in range(tile // DH):
+                cols = slice(h * DH, (h + 1) * DH)
+                q = src[t, :, :, cols].reshape(2 * rows, DH)
+                scores = lax.dot_general(
+                    q, k_ref[:, columns(t, DH, h * DH)], (((1,), (1,)), ((), ())),
+                    preferred_element_type=jnp.float32,
+                )
+                weights = (silu(scores * DH ** (-0.5)) * mask[half]).astype(jnp.bfloat16)
+                out = jnp.dot(
+                    weights, v_ref[:, columns(t, DH, h * DH)], preferred_element_type=jnp.float32
+                ).reshape(2, rows, DH)
+                if half == 0:
+                    part[t, :, :, cols] = out
+                else:
+                    s4[t, :, :, cols] = out.astype(jnp.bfloat16)
+            if half == 1:
+                copy4(t).start()
+
+    @pl.when(step < n_tiles)
+    def _():
+        t = step
+        chunk = min(512, depth)
+        for d in range(depth // chunk):
+            block = w_ref[d * chunk:(d + 1) * chunk]
+            flat = jnp.concatenate([block[:, j, :] for j in range(4)], axis=1)
+            term = jnp.dot(
+                tok_ref[:, d * chunk:(d + 1) * chunk], flat, preferred_element_type=jnp.float32
+            )
+            if d == 0:
+                acc[...] = term
+            else:
+                acc[...] += term
+        for xx in range(2):
+            s1[t, xx] = acc[quarter(xx, 1 - c), :].astype(jnp.bfloat16)
+        copy1(t).start()
+        for xx in range(2):
+            mine[t, xx] = acc[quarter(xx, c), :].astype(jnp.bfloat16)
+
+
+def fused_history(tokens, w_qkvu, k_cache, v_cache, vis_start, vis_end):
+    cand, depth = tokens.shape
+    width = w_qkvu.shape[2]
+    events = k_cache.shape[0]
+    n_tiles = width // TILE
+    rows = cand // 4
+    lo = jnp.broadcast_to(vis_start[:, None], (cand, 128))
+    hi = jnp.broadcast_to(vis_end[:, None], (cand, 128))
+
+    def whole(shape):
+        return pl.BlockSpec(shape, lambda i: (0, 0), pipeline_mode=pl.Buffered(1))
+
+    def half(extra, cols):
+        return pltpu.VMEM((n_tiles,) + extra + (rows, cols), jnp.bfloat16)
+
+    return pl.pallas_call(
+        functools.partial(history_kernel, n_tiles),
+        grid=(n_tiles + 5,),
+        in_specs=[
+            whole((cand, depth)),
+            pl.BlockSpec((depth, 4, TILE), lambda i: (0, 0, jnp.minimum(i, n_tiles - 1))),
+            whole((events, width)),
+            whole((events, width)),
+            whole((cand, 128)),
+            whole((cand, 128)),
+        ],
+        out_specs=[whole((rows, width)), whole((rows, width))],
+        out_shape=[
+            jax.ShapeDtypeStruct((rows, width), jnp.float32),
+            jax.ShapeDtypeStruct((rows, width), jnp.bfloat16),
+        ],
+        scratch_shapes=[
+            pltpu.VMEM((cand, 4 * TILE), jnp.float32),
+            pltpu.VMEM((2, 2 * rows, events), jnp.float32),
+            half((2,), 4 * TILE),
+            half((2,), 4 * TILE), half((2,), 4 * TILE),
+            half((2,), TILE), half((2,), TILE),
+            half((), 3 * TILE), half((), 3 * TILE),
+            half((2,), TILE), half((2,), TILE),
+            half((), 2 * TILE),
+            half((2,), TILE), half((2,), TILE),
+            pltpu.VMEM((n_tiles, 2, rows, TILE), jnp.float32),
+            half((), TILE), half((), TILE),
+            pltpu.SemaphoreType.DMA((6, n_tiles)),
+            pltpu.SemaphoreType.DMA((6, n_tiles)),
+        ],
+        compiler_params=pltpu.CompilerParams(
+            vmem_limit_bytes=62 << 20, collective_id=0, has_side_effects=True
+        ),
+        name="history",
+    )(tokens, w_qkvu, k_cache, v_cache, lo, hi)
+
+
+def local_fused(tokens, w_qkvu, k_cache, v_cache, w_out, vis_start, vis_end):
+    cand_total = tokens.shape[0]
+    head_count = lax.axis_size("head")
+    local_width = w_qkvu.shape[2]
+    full_width = local_width * head_count
+    attended, gate = fused_history(tokens, w_qkvu, k_cache, v_cache, vis_start, vis_end)
+    local_mean = jnp.mean(attended, axis=1)
+    off = attended - local_mean[:, None]
+    local_sq = jnp.sum(off * off, axis=1)
+    both = lax.all_gather(jnp.stack([local_mean, local_sq]), "head", axis=0)
+    mean = jnp.mean(both[:, 0], axis=0)
+    shift = both[:, 0] - mean[None]
+    spread = jnp.sum(both[:, 1] + local_width * shift * shift, axis=0)
+    normed = (attended - mean[:, None]) * lax.rsqrt(spread / full_width + epsilon)[:, None]
+    gated_rows = (normed * gate.astype(jnp.float32)).astype(jnp.bfloat16)
+    gathered = lax.all_gather(gated_rows, "hist", axis=0, tiled=True)
+    out_count = cand_total // head_count
+    out_first = lax.axis_index("head") * out_count
+    whole_out = jnp.dot(gathered, w_out, preferred_element_type=jnp.float32)
+    summed_out = lax.psum_scatter(
+        whole_out.astype(jnp.bfloat16), "head", scatter_dimension=0, tiled=True
+    ).astype(jnp.float32)
+    residual = lax.dynamic_slice_in_dim(tokens, out_first, out_count, 0).astype(jnp.float32)
+    return (residual + summed_out).astype(jnp.bfloat16)
+
+
 def solution(mesh):
     in_specs = (
         P("groups", "hist"),
@@ -91,4 +341,5 @@
         P("groups"),
     )
     out_specs = P(("groups", "head"), "hist")
-    return jax.shard_map(local, mesh=mesh, in_specs=in_specs, out_specs=out_specs, check_vma=False)
+    body = local_fused if mesh.shape["hist"] == 4 else local
+    return jax.shard_map(body, mesh=mesh, in_specs=in_specs, out_specs=out_specs, check_vma=False)

time: 368 us -> 209 us (0.57)
  waiting for transfers between devices: 213 us -> 67 us
  Pallas kernels: 0 us -> 97.5 us
  local copies, waits for them, and re-layouts: 58.6 us -> 3.04 us
  matrix products: 47.3 us -> 9.87 us
  other arithmetic: 16.3 us -> 6.2 us
  blocking collectives: 16.3 us -> 9.14 us
    pallas_call x0 -> x1, Pallas kernels: none -> 97.5 us  [fused_history(): pl.pallas_call(functools.partial(history_kernel, n_tiles), grid=(n_tiles...]
    psum x1 -> x0, waiting for transfers between devices: 86.5 us -> none  [local(): lax.psum(whole_out.astype(jnp.bfloat16), 'head').astype(jnp.float32)]
    all_gather x3 -> x1, waiting for transfers between devices: 65.8 us -> 23.1 us  [local_fused(): gathered = lax.all_gather(gated_rows, 'hist', axis=0, tiled=True)]
    unnamed x10 -> x4, local copies, waits for them, and re-layouts: 39.8 us -> 0.01 us
    dot_general x3 -> x1, matrix products: 47.3 us -> 9.87 us  [local_fused(): whole_out = jnp.dot(gathered, w_out, preferred_element_type=jnp.float32)]
    psum x2 -> x0, blocking collectives: 16.3 us -> none  [the longest x1 9.66 us: local(): row_sum = lax.psum(jnp.sum(attended, axis=1), 'head')]
    reduce_scatter x1, waiting for transfers between devices: 60.2 us -> 43.9 us  [local_fused(): lax.psum_scatter(whole_out.astype(jnp.bfloat16), 'head', scatter_dimensio...]
    all_gather x1 -> x0, local copies, waits for them, and re-layouts: 12.5 us -> none  [local(): lax.all_gather(v_cache, 'hist', axis=0, tiled=True)]
  transfers between devices with their start and end apart: 5 -> 2, of which waited for: 4 -> 2; matrix products, arithmetic and copies ran while one was open for 25% -> 0% of each run, Pallas kernels for 0% -> 0%
where the time goes in v1:
time: 209 us; the launch traced here: 206 us
  Pallas kernels  97.5 us (47%)
  waiting for transfers between devices  67 us (32%)
  between operations  13.4 us (6%)
  matrix products  9.87 us (5%)
  blocking collectives  9.14 us (4%)
  other arithmetic  6.2 us (3%)
  local copies, waits for them, and re-layouts  3.04 us (1%)
    pallas_call x1, Pallas kernels, fused_history(): pl.pallas_call(functools.partial(history_kernel, n_tiles), grid=(n_tiles...  97.5 us
    reduce_scatter x1, waiting for transfers between devices, local_fused(): lax.psum_scatter(whole_out.astype(jnp.bfloat16), 'head', scatter_dimensio...  43.9 us
    all_gather x1, waiting for transfers between devices, local_fused(): gathered = lax.all_gather(gated_rows, 'hist', axis=0, tiled=True)  23.1 us
    dot_general x1, matrix products, local_fused(): whole_out = jnp.dot(gathered, w_out, preferred_element_type=jnp.float32)  9.87 us
    all_gather x1, blocking collectives, local_fused(): both = lax.all_gather(jnp.stack([local_mean, local_sq]), 'head', axis=0)  9.14 us
  transfers between devices with their start and end apart: 2, of which 2 were waited for; matrix products, arithmetic and copies ran while one was open for 0% of the time, Pallas kernels for 0%

profile of v1, /device:TPU:7, one launch (start us, length us, event | category | flops | bytes accessed | tf_op | source)
XLA Modules:
  0.0 206.4 jit_solution(2670723386616943910)
XLA Ops:
  6.5 0.0 all-gather.4.cloned.1.call-start
  6.5 1.5 broadcast_in_dim.4.lo_ref
  8.1 1.5 broadcast_in_dim.5.hi_ref
  9.6 97.5 %history.1 = (f32[128,2048]{1,0:T(8,128)}, bf16[128,2048]{1,0:T(8,128)(2,1)}) custom-call(bf16[512,2048]{1,0:T(8,128)(2,1)} %tok_ref.1, bf16[2048,4,2048]{2,1,0:T(4,128)(2,1)} %w_ref.1, bf16[512,2048]{1,0:T(8,128)(2,1)} %k_ref.1, bf16[512,2048]{1,0:T(8,128)(2,1)} %v_ref.1, s32[512,128]{1,0:T(8,128)} %broadcast_in_dim.4.lo_ref, s32[512,128]{1,0:T(8,128)} %broadcast_in_dim.5.hi_ref), custom_call_target="tpu_custom_call" | custom-call | tf_op jit(solution)/shard_map/history/pallas_call | solution.py:269
  107.1 0.0 copy-start
  107.1 0.0 copy-start.1
  107.1 1.5 reduce_sum.36
  108.6 1.5 multiply_reduce_fusion
  110.1 9.1 %all-gather.1 = f32[4,2,128]{2,1,0:T(2,128)S(1)} all-gather(f32[1,2,128]{2,1,0:T(2,128)S(1)} %maximum_bitcast_fusion), channel_id=2, replica_groups=mesh['groups'=2,'head'=4,'hist'=4] {'head'}, dimensions={0}, use_global_device_ids=true | all-gather | bytes 5120 | tf_op jit(solution)/shard_map/all_gather | solution.py:316
  119.3 0.0 copy-done
  119.3 0.0 copy-done.1
  119.3 1.0 multiply_convert_fusion
  120.3 0.0 all-gather.4.cloned.1.call-update
  120.4 0.2 reduce-scatter.2.cloned.1.call-start
  120.6 23.1 %all-gather.4.cloned.1.call-done = bf16[512,2048]{1,0:T(8,128)(2,1)} async-done(((bf16[128,2048]{1,0:T(8,128)(2,1)}), bf16[512,2048]{1,0:T(8,128)(2,1)}) %all-gather.4.cloned.1.call-update) | async-done | bytes 2097168 | tf_op jit(solution)/shard_map/all_gather | solution.py:322
  143.6 9.9 %convolution_convert_fusion = bf16[512,2048]{1,0:T(8,128)(2,1)} fusion(bf16[512,2048]{1,0:T(8,128)(2,1)} %all-gather.4.cloned.1.call-done, bf16[2048,2048]{1,0:T(8,128)(2,1)} %param.11), kind=kOutput, calls=%fused_computation | convolution fusion | flops 4296015872 | bytes 12582912 | tf_op jit(solution)/shard_map/dot_general | solution.py:325
  153.5 0.0 reduce-scatter.2.cloned.1.call-update
  153.5 43.9 %reduce-scatter.2.cloned.1.call-done = bf16[128,2048]{1,0:T(8,128)(2,1)} async-done(((bf16[512,2048]{1,0:T(8,128)(2,1)}), bf16[128,2048]{1,0:T(8,128)(2,1)}) %reduce-scatter.2.cloned.1.call-update) | async-done | bytes 524304 | tf_op jit(solution)/shard_map/reduce_scatter | solution.py:326
  197.4 2.1 %add_convert_fusion = bf16[128,2048]{1,0:T(8,128)(2,1)} fusion(bf16[128,2048]{1,0:T(8,128)(2,1)} %reduce-scatter.2.cloned.1.call-done, bf16[512,2048]{1,0:T(8,128)(2,1)} %tok_ref.1, s32[]{:T(128)S(6)} %select_n.3), kind=kLoop, calls=%fused_computation.1 | loop fusion | flops 1048576 | bytes 1572868 | tf_op jit(solution)/shard_map/convert_element_type | solution.py:330
  (6 shorter events, 0.1 us)
Async XLA Ops:
  6.5 137.1 %all-gather.4.cloned.1.call-start = ((), (), s32[]{:S(2)}) async-start(), calls=%async_computation.1 | async-start | bytes 2621440 | tf_op jit(solution)/shard_map/all_gather | solution.py:322
  107.1 12.2 %copy-start = (f32[128,2048]{1,0:T(8,128)S(1)}, f32[128,2048]{1,0:T(8,128)}, u32[]{:S(2)}) copy-start(f32[128,2048]{1,0:T(8,128)} %get-tuple-element.7) | copy-start | bytes 3145732
  107.1 12.2 %copy-start.1 = (bf16[128,2048]{1,0:T(8,128)(2,1)S(1)}, bf16[128,2048]{1,0:T(8,128)(2,1)}, u32[]{:S(2)}) copy-start(bf16[128,2048]{1,0:T(8,128)(2,1)} %get-tuple-element.8) | copy-start | bytes 1572868
  120.4 77.1 %reduce-scatter.2.cloned.1.call-start = ((), (), s32[]{:S(2)}) async-start(), calls=%async_computation.2 | async-start | bytes 2621440 | tf_op jit(solution)/shard_map/reduce_scatter | solution.py:326
Sparse Core Ops, SparseCore 0:
  120.5 23.1 all-gather.3
  153.6 43.7 reduce-scatter.1

commit v2 on v1

--- a/solution.py
+++ b/solution.py
@@ -304,30 +304,194 @@
     )(tokens, w_qkvu, k_cache, v_cache, lo, hi)
 
 
+def output_kernel(
+    att_ref, gate_ref, w_hbm, tok_hbm, out_ref,
+    w_out, res, stat, got, units, own, near, far, relay, passed,
+    load_sem, st_s, st_r, g_s, g_r, u_s, near_r, far_r, relay_r,
+):
+    mesh_id = pl.DeviceIdType.MESH
+    me = lax.axis_index("hist")
+    z = lax.axis_index("head")
+    x = me // 2
+    c = me % 2
+    partner = 2 * x + (1 - c)
+    across = 2 * (1 - x) + c
+    peer = 2 * (z // 2) + 1 - z % 2
+    inner = (z // 2) != (z % 2)
+    rows, width = att_ref.shape
+    piece = out_ref.shape[1] // 2
+    quarters = (me, partner, across, 2 * (1 - x) + (1 - c))
+
+    load_w = pltpu.make_async_copy(w_hbm, w_out, load_sem.at[0])
+    load_w.start()
+    load_t = pltpu.make_async_copy(
+        tok_hbm.at[pl.ds(pl.multiple_of(z * rows, rows), rows), :], res, load_sem.at[1]
+    )
+    load_t.start()
+
+    barrier = pltpu.get_barrier_semaphore()
+    for other in (partner, across):
+        pl.semaphore_signal(barrier, inc=1, device_id={"hist": other}, device_id_type=mesh_id)
+    for k in range(1, 4):
+        pl.semaphore_signal(
+            barrier, inc=1, device_id={"head": (z + k) % 4}, device_id_type=mesh_id
+        )
+    pl.semaphore_wait(barrier, 5)
+
+    att = att_ref[...]
+    local_mean = jnp.sum(att, axis=1, keepdims=True) / width
+    off = att - local_mean
+    local_sq = jnp.sum(off * off, axis=1, keepdims=True)
+    lane = lax.broadcasted_iota(jnp.int32, (rows, 128), 1)
+    stat[0] = jnp.where(lane < 64, local_mean, local_sq)
+    stat_copies = []
+    for k in range(1, 4):
+        cp = pltpu.make_async_remote_copy(
+            src_ref=stat.at[0], dst_ref=stat.at[k], send_sem=st_s.at[k - 1],
+            recv_sem=st_r.at[k - 1], device_id={"head": (z + k) % 4}, device_id_type=mesh_id,
+        )
+        cp.start()
+        stat_copies.append(cp)
+    for cp in stat_copies:
+        cp.wait()
+    means = [stat[k, :, 0:1] for k in range(4)]
+    mean = (means[0] + means[1] + means[2] + means[3]) / 4
+    spread = jnp.zeros_like(mean)
+    for k in range(4):
+        shift = means[k] - mean
+        spread = spread + stat[k, :, 127:128] + width * shift * shift
+    inv = lax.rsqrt(spread / (4 * width) + epsilon)
+    got[0] = ((att_ref[...] - mean) * inv * gate_ref[...].astype(jnp.float32)).astype(jnp.bfloat16)
+
+    def gather(k, src, dst, target):
+        return pltpu.make_async_remote_copy(
+            src_ref=got.at[src], dst_ref=got.at[dst], send_sem=g_s.at[k], recv_sem=g_r.at[k],
+            device_id={"hist": target}, device_id_type=mesh_id,
+        )
+
+    to_across = gather(1, 0, 2, across)
+    to_across.start()
+    to_partner = gather(0, 0, 1, partner)
+    to_partner.start()
+    pass_on = gather(2, 2, 3, partner)
+
+    def unit_copy(i, p, src, dst, recv_sem, target):
+        return pltpu.make_async_remote_copy(
+            src_ref=src, dst_ref=dst, send_sem=u_s.at[i, p], recv_sem=recv_sem,
+            device_id={"head": target}, device_id_type=mesh_id,
+        )
+
+    def is_far(i):
+        return (quarters[i] // 2) != (z // 2)
+
+    def near_copy(i, p):
+        return unit_copy(i, p, units.at[i, p], near.at[p], near_r.at[p], peer)
+
+    def relay_copy(i, p):
+        slot = quarters[i] % 2
+        return unit_copy(i, p, units.at[i, p], relay.at[slot, p], relay_r.at[slot, p], peer)
+
+    def far_copy(i, p):
+        r = quarters[i]
+        return unit_copy(i, p, passed.at[r % 2, p], far.at[p], far_r.at[p], r)
+
+    def multiply(pair, p):
+        both = got[2 * pair:2 * pair + 2].reshape(2 * rows, width)
+        acc = jnp.dot(
+            both, w_out[:, p * piece:(p + 1) * piece], preferred_element_type=jnp.float32
+        )
+        for k in range(2):
+            i = 2 * pair + k
+            term = acc[k * rows:(k + 1) * rows]
+            units[i, p] = term.astype(jnp.bfloat16)
+
+            @pl.when(quarters[i] == z)
+            def _():
+                own[p] = term
+
+            @pl.when(quarters[i] == peer)
+            def _():
+                near_copy(i, p).start()
+
+            @pl.when(is_far(i) & jnp.logical_not(inner))
+            def _():
+                relay_copy(i, p).start()
+
+    def forward(pair):
+        for p in range(2):
+            for k in range(2):
+                i = 2 * pair + k
+
+                @pl.when(is_far(i) & inner)
+                def _():
+                    relay_copy(i, p).wait_recv()
+                    slot = quarters[i] % 2
+                    total = units[i, p].astype(jnp.float32) + relay[slot, p].astype(jnp.float32)
+                    passed[slot, p] = total.astype(jnp.bfloat16)
+                    far_copy(i, p).start()
+
+    load_w.wait()
+    to_partner.wait()
+    multiply(0, 0)
+    multiply(0, 1)
+    to_across.wait()
+    pass_on.start()
+    pass_on.wait()
+    multiply(1, 0)
+    forward(0)
+    multiply(1, 1)
+    forward(1)
+    load_t.wait()
+    for p in range(2):
+        near_copy(0, p).wait_recv()
+        far_copy(0, p).wait_recv()
+        total = own[p] + near[p].astype(jnp.float32) + far[p].astype(jnp.float32)
+        cols = slice(p * piece, (p + 1) * piece)
+        out_ref[:, cols] = (res[:, cols].astype(jnp.float32) + total).astype(jnp.bfloat16)
+    for i in range(4):
+        for p in range(2):
+            @pl.when(quarters[i] != z)
+            def _():
+                near_copy(i, p).wait_send()
+
+
+def fused_output(attended, gate, w_out, tokens):
+    rows, width = attended.shape
+    cols = w_out.shape[1]
+    piece = cols // 2
+    vmem = pl.BlockSpec(memory_space=pltpu.VMEM)
+    anywhere = pl.BlockSpec(memory_space=pl.ANY)
+    dma = pltpu.SemaphoreType.DMA
+
+    def slots(*lead):
+        return pltpu.VMEM(lead + (rows, piece), jnp.bfloat16)
+
+    return pl.pallas_call(
+        output_kernel,
+        in_specs=[vmem, vmem, anywhere, anywhere],
+        out_specs=vmem,
+        out_shape=jax.ShapeDtypeStruct((rows, cols), jnp.bfloat16),
+        scratch_shapes=[
+            pltpu.VMEM((width, cols), jnp.bfloat16),
+            pltpu.VMEM((rows, cols), jnp.bfloat16),
+            pltpu.VMEM((4, rows, 128), jnp.float32),
+            pltpu.VMEM((4, rows, width), jnp.bfloat16),
+            slots(4, 2),
+            pltpu.VMEM((2, rows, piece), jnp.float32),
+            slots(2), slots(2), slots(2, 2), slots(2, 2),
+            dma((2,)), dma((3,)), dma((3,)), dma((3,)), dma((3,)),
+            dma((4, 2)), dma((2,)), dma((2,)), dma((2, 2)),
+        ],
+        compiler_params=pltpu.CompilerParams(
+            vmem_limit_bytes=60 << 20, collective_id=1, has_side_effects=True
+        ),
+        name="output",
+    )(attended, gate, w_out, tokens)
+
+
 def local_fused(tokens, w_qkvu, k_cache, v_cache, w_out, vis_start, vis_end):
-    cand_total = tokens.shape[0]
-    head_count = lax.axis_size("head")
-    local_width = w_qkvu.shape[2]
-    full_width = local_width * head_count
     attended, gate = fused_history(tokens, w_qkvu, k_cache, v_cache, vis_start, vis_end)
-    local_mean = jnp.mean(attended, axis=1)
-    off = attended - local_mean[:, None]
-    local_sq = jnp.sum(off * off, axis=1)
-    both = lax.all_gather(jnp.stack([local_mean, local_sq]), "head", axis=0)
-    mean = jnp.mean(both[:, 0], axis=0)
-    shift = both[:, 0] - mean[None]
-    spread = jnp.sum(both[:, 1] + local_width * shift * shift, axis=0)
-    normed = (attended - mean[:, None]) * lax.rsqrt(spread / full_width + epsilon)[:, None]
-    gated_rows = (normed * gate.astype(jnp.float32)).astype(jnp.bfloat16)
-    gathered = lax.all_gather(gated_rows, "hist", axis=0, tiled=True)
-    out_count = cand_total // head_count
-    out_first = lax.axis_index("head") * out_count
-    whole_out = jnp.dot(gathered, w_out, preferred_element_type=jnp.float32)
-    summed_out = lax.psum_scatter(
-        whole_out.astype(jnp.bfloat16), "head", scatter_dimension=0, tiled=True
-    ).astype(jnp.float32)
-    residual = lax.dynamic_slice_in_dim(tokens, out_first, out_count, 0).astype(jnp.float32)
-    return (residual + summed_out).astype(jnp.bfloat16)
+    return fused_output(attended, gate, w_out, tokens)
 
 
 def solution(mesh):
@@ -341,5 +505,5 @@
         P("groups"),
     )
     out_specs = P(("groups", "head"), "hist")
-    body = local_fused if mesh.shape["hist"] == 4 else local
+    body = local_fused if mesh.shape["hist"] == 4 and mesh.shape["head"] == 4 else local
     return jax.shard_map(body, mesh=mesh, in_specs=in_specs, out_specs=out_specs, check_vma=False)

time: 209 us -> 162 us (0.78); the launches traced: 206 us -> 162 us
  waiting for transfers between devices: 67 us -> 0 us
  Pallas kernels: 97.5 us -> 157 us
  between operations: 13.4 us -> 0.02 us
  matrix products: 9.87 us -> 0 us
  blocking collectives: 9.14 us -> 0 us
  other arithmetic: 6.2 us -> 0 us
    pallas_call x0 -> x1, Pallas kernels: none -> 59.8 us  [fused_output(): pl.pallas_call(output_kernel, in_specs=[vmem, vmem, anywhere, anywhere],...]
    reduce_scatter x1 -> x0, waiting for transfers between devices: 43.9 us -> none  [local_fused(): lax.psum_scatter(whole_out.astype(jnp.bfloat16), 'head', scatter_dimensio...]
    all_gather x1 -> x0, waiting for transfers between devices: 23.1 us -> none  [local_fused(): gathered = lax.all_gather(gated_rows, 'hist', axis=0, tiled=True)]
    dot_general x1 -> x0, matrix products: 9.87 us -> none  [local_fused(): whole_out = jnp.dot(gathered, w_out, preferred_element_type=jnp.float32)]
    all_gather x1 -> x0, blocking collectives: 9.14 us -> none  [local_fused(): both = lax.all_gather(jnp.stack([local_mean, local_sq]), 'head', axis=0)]
    convert_element_type x2 -> x0, other arithmetic: 3.17 us -> none  [the longest x1 2.12 us: local_fused(): return (residual + summed_out).astype(jnp.bfloat16)]
    reduce_sum x4 -> x0, other arithmetic: 3 us -> none  [the longest x1 1.48 us: local_fused(): local_mean = jnp.mean(attended, axis=1)]
  transfers between devices with their start and end apart: 2 -> 0, of which waited for: 2 -> 0; matrix products, arithmetic and copies ran while one was open for 0% -> 0% of each run, Pallas kernels for 0% -> 0%
where the time goes in v2:
time: 162 us
  Pallas kernels  157 us (97%)
  local copies, waits for them, and re-layouts  4.92 us (3%)
    pallas_call x1, Pallas kernels, fused_history(): pl.pallas_call(functools.partial(history_kernel, n_tiles), grid=(n_tiles...  97.5 us
    pallas_call x1, Pallas kernels, fused_output(): pl.pallas_call(output_kernel, in_specs=[vmem, vmem, anywhere, anywhere],...  59.8 us

profile of v2, /device:TPU:7, one launch (start us, length us, event | category | flops | bytes accessed | tf_op | source)
XLA Modules:
  0.0 162.3 jit_solution(11577127898826761551)
XLA Ops:
  0.0 1.5 broadcast_in_dim.4.lo_ref
  1.5 1.5 broadcast_in_dim.5.hi_ref
  3.0 97.5 %history.1 = (f32[128,2048]{1,0:T(8,128)}, bf16[128,2048]{1,0:T(8,128)(2,1)}) custom-call(bf16[512,2048]{1,0:T(8,128)(2,1)} %tok_hbm.1, bf16[2048,4,2048]{2,1,0:T(4,128)(2,1)} %w_ref.1, bf16[512,2048]{1,0:T(8,128)(2,1)} %k_ref.1, bf16[512,2048]{1,0:T(8,128)(2,1)} %v_ref.1, s32[512,128]{1,0:T(8,128)} %broadcast_in_dim.4.lo_ref, s32[512,128]{1,0:T(8,128)} %broadcast_in_dim.5.hi_ref), custom_call_target="tpu_custom_call" | custom-call | tf_op jit(solution)/shard_map/history/pallas_call | solution.py:269
  100.5 59.8 %output.1 = bf16[128,2048]{1,0:T(8,128)(2,1)} custom-call(f32[128,2048]{1,0:T(8,128)} %get-tuple-element.7.att_ref, bf16[128,2048]{1,0:T(8,128)(2,1)} %get-tuple-element.8.gate_ref, bf16[2048,2048]{1,0:T(8,128)(2,1)} %w_hbm.1, bf16[512,2048]{1,0:T(8,128)(2,1)} %tok_hbm.1), custom_call_target="tpu_custom_call" | custom-call | tf_op jit(solution)/shard_map/output/pallas_call | solution.py:469
  160.4 1.9 %copy.9 = bf16[128,2048]{1,0:T(8,128)(2,1)} copy(bf16[128,2048]{1,0:T(8,128)(2,1)} %output.1) | data formatting | bytes 1048576
